TPU v7x, 512 devices: a whole 4x8x8 slice. The times are simulated.
512 devices in a mesh: ev: 32 (over x, y_lo, core), ch: 16 (over y_hi, z).
Axes of the slice: x: 4, y: 8 (y_hi: 2, y_lo: 4; y = y_hi * 4 + y_lo), z: 8, core: 2. Of those that a mesh axis runs over, the one named last changes fastest.
Arguments:
- spectra: float32 [512, 16, 65536], P('ev', None, 'ch'), as said below
- tile_mask: int32 [512, 512], P('ev', 'ch'), may hold values 0 or 1
- source_init: float32 [512, 16], P('ev'), may hold values from -6 to 6
- site_init: float32 [16, 65536], P(None, 'ch'), may hold values from -6 to 6
- event_pos: float32 [3, 512], P(None, 'ev'), may hold values from 5 to 50
- channel_pos: float32 [2, 65536], P(None, 'ch'), may hold values from 0 to 50
- atten: float32 [16], replicated, may hold values from 0.02 to 0.3
Outputs:
- source: float32 [512, 16], P('ev')
- site: float32 [16, 65536], P(None, 'ch')
Inputs may be any that keep to these rules, and one draw needn't show every extreme that they name: spectra are log amplitudes of order one to a few, with outliers. `tile_mask`: 0 marks an event invalid on a whole tile of 128 channels.
All inputs are finite; a program needn't handle non-finite values. No bound on the sum of `tile_mask` on one device may be relied on, other than what follows from the above.
Results may differ from a plain program's by a relative error of at most 0.0001.
Values sent between devices are 32-bit elements; how exact they have to be, the bound alone decides.
A program may use at most 64 MiB of HBM per device.

v0:
```python
import jax
import jax.numpy as jnp
from jax import lax
from jax.sharding import PartitionSpec as P

ITERS = 2


def on_device(spectra, tile_mask, source_init, site_init, event_pos, channel_pos, atten):
    ev_n, freqs, ch_n = spectra.shape
    total_ch = ch_n * lax.axis_size("ch")
    valid = jnp.repeat(tile_mask, 128, axis=1).astype(jnp.float32)[:, None, :]
    count_part = jnp.sum(valid)
    east = event_pos[0][:, None] - channel_pos[0][None, :]
    north = event_pos[1][:, None] - channel_pos[1][None, :]
    depth = event_pos[2][:, None]
    travel = jnp.sqrt(east * east + north * north + depth * depth) / 3.0
    path = atten[None, :, None] * travel[:, None, :]
    source = source_init
    site = site_init
    for step in range(ITERS):
        resid = spectra - source[:, :, None] - site[None, :, :] + path
        abs_part = jnp.sum(valid * jnp.abs(resid), axis=(0, 2))
        absum, count = lax.psum((abs_part, count_part), ("ev", "ch"))
        delta = 1.345 * (1.2533 * absum / jnp.maximum(count, 1.0) + 1e-05)
        limit = delta[None, :, None]
        weight = limit / jnp.maximum(jnp.abs(resid), limit) * valid
        product = weight * resid
        src_num, src_den = lax.psum((jnp.sum(product, axis=2), jnp.sum(weight, axis=2)), "ch")
        site_num = jnp.sum(product, axis=0)
        site_den = jnp.sum(weight, axis=0)
        site_num, site_den = lax.psum((site_num, site_den), "ev")
        site = site + 0.5 * site_num / (site_den + 1.0)
        source = source + 0.5 * src_num / (src_den + 1.0)
        shift = lax.psum(jnp.sum(site, axis=1), "ch") / total_ch
        site = site - shift[:, None]
        source = source + shift[None, :]
    return (source, site)


def solution(mesh):
    in_specs = (
        P("ev", None, "ch"),
        P("ev", "ch"),
        P("ev", None),
        P(None, "ch"),
        P(None, "ev"),
        P(None, "ch"),
        P(),
    )
    out_specs = (P("ev", None), P(None, "ch"))
    return jax.shard_map(
        on_device, mesh=mesh, in_specs=in_specs, out_specs=out_specs, check_vma=False
    )
```

profile of v0, /device:TPU:1, one launch (start us, length us, event | category | flops | bytes accessed | tf_op | source)
XLA Modules:
  0.0 970.5 jit_solution(700504949465934503)
XLA Ops:
  7.2 0.0 copy-start.2
  7.2 0.0 copy-start
  7.2 0.0 copy-start.1
  7.2 0.0 all-reduce.10.cloned.1.call-start
  7.2 0.8 slice_bitcast_fusion.1
  8.0 0.7 convert_element_type.13
  8.7 0.9 fusion.8
  9.6 0.1 broadcast_in_dim.2
  9.7 0.2 copy.11
  9.9 0.2 sqrt_multiply_fusion
  10.1 3.4 multiply_reduce_fusion.1
  13.5 0.7 broadcast_reduce_fusion
  14.2 106.1 %all-reduce = (f32[16]{0:T(128)S(1)}, f32[]{:T(128)}) all-reduce(f32[16]{0:T(128)S(1)} %multiply_reduce_fusion.1, f32[]{:T(128)} %broadcast_reduce_fusion), channel_id=1, replica_groups=mesh['ev'=32,'ch'=16] {'ev','ch'}, use_global_device_ids=true, to_apply=%region_1.0 | all-reduce | flops 17 | bytes 136 | tf_op jit(solution)/shard_map/psum | solution.py:24
  121.0 0.0 copy-done.2
  121.0 0.0 copy-done
  121.0 0.0 copy-done.1
  121.0 5.4 fusion.4
  126.4 0.0 all-reduce.10.cloned.1.call-update
  126.4 0.0 all-reduce.8.cloned.1.call-start
  126.5 275.8 %all-reduce.10.cloned.1.call-done = (f32[16,4096]{1,0:T(8,128)}, f32[16,4096]{1,0:T(8,128)}) async-done(((f32[16,4096]{1,0:T(8,128)}, f32[16,4096]{1,0:T(8,128)}), (f32[16,4096]{1,0:T(8,128)}, f32[16,4096]{1,0:T(8,128)})) %all-reduce.10.cloned.1.call-update) | async-done | bytes 524304 | tf_op jit(solution)/shard_map/psum | solution.py:32
  402.2 1.2 fusion.7
  403.4 82.8 %all-reduce.4 = (f32[16,16]{1,0:T(8,128)S(1)}, f32[16,16]{1,0:T(8,128)S(1)}, f32[16]{0:T(128)S(1)}) all-reduce(f32[16,16]{1,0:T(8,128)S(1)} %get-tuple-element.9, f32[16,16]{1,0:T(8,128)S(1)} %get-tuple-element.5, f32[16]{0:T(128)S(1)} %get-tuple-element.24), channel_id=1, replica_groups=mesh['ev'=32,'ch'=16] {'ch'}, use_global_device_ids=true, to_apply=%region_7.0 | all-reduce | flops 528 | bytes 4224 | tf_op jit(solution)/shard_map/psum | solution.py:29
  486.2 0.1 broadcast_subtract_fusion.1
  486.3 3.3 multiply_reduce_fusion
  489.7 108.8 %psum.101 = f32[16]{0:T(128)S(1)} all-reduce(f32[16]{0:T(128)S(1)} %multiply_reduce_fusion), channel_id=1, replica_groups=mesh['ev'=32,'ch'=16] {'ev','ch'}, use_global_device_ids=true, to_apply=%region_15.0 | all-reduce | flops 16 | bytes 128 | tf_op jit(solution)/shard_map/psum | solution.py:24
  598.4 5.4 fusion.2
  603.8 0.0 all-reduce.8.cloned.1.call-update
  603.8 274.4 %all-reduce.8.cloned.1.call-done = (f32[16,4096]{1,0:T(8,128)}, f32[16,4096]{1,0:T(8,128)}) async-done(((f32[16,4096]{1,0:T(8,128)}, f32[16,4096]{1,0:T(8,128)}), (f32[16,4096]{1,0:T(8,128)}, f32[16,4096]{1,0:T(8,128)})) %all-reduce.8.cloned.1.call-update) | async-done | bytes 524304 | tf_op jit(solution)/shard_map/psum | solution.py:32
  878.2 1.2 fusion.6
  879.4 82.8 %all-reduce.3 = (f32[16,16]{1,0:T(8,128)S(1)}, f32[16,16]{1,0:T(8,128)S(1)}, f32[16]{0:T(128)S(1)}) all-reduce(f32[16,16]{1,0:T(8,128)S(1)} %get-tuple-element.7, f32[16,16]{1,0:T(8,128)S(1)} %get-tuple-element.3, f32[16]{0:T(128)S(1)} %get-tuple-element.22), channel_id=1, replica_groups=mesh['ev'=32,'ch'=16] {'ch'}, use_global_device_ids=true, to_apply=%region_19.0 | all-reduce | flops 528 | bytes 4224 | tf_op jit(solution)/shard_map/psum | solution.py:29
  962.3 0.8 broadcast_subtract_fusion
  963.1 0.6 add_add_fusion
  (5 shorter events, 0.0 us)
Async XLA Ops:
  7.2 113.8 %copy-start.2 = (f32[16]{0:T(128)S(1)}, f32[16]{0:T(128)}, u32[]{:S(2)}) copy-start(f32[16]{0:T(128)} %param.13) | copy-start | bytes 196
  7.2 113.8 %copy-start = (f32[16,4096]{1,0:T(8,128)S(1)}, f32[16,4096]{1,0:T(8,128)}, u32[]{:S(2)}) copy-start(f32[16,4096]{1,0:T(8,128)} %param.10) | copy-start | bytes 786436
  7.2 113.8 %copy-start.1 = (f32[16,16]{1,0:T(8,128)S(1)}, f32[16,16]{1,0:T(8,128)}, u32[]{:S(2)}) copy-start(f32[16,16]{1,0:T(8,128)} %param.9) | copy-start | bytes 3076
  7.2 395.0 %all-reduce.10.cloned.1.call-start = ((), (), s32[]{:S(2)}) async-start(), calls=%async_computation.1 | async-start | bytes 1048576 | tf_op jit(solution)/shard_map/psum | solution.py:32
  126.4 751.8 %all-reduce.8.cloned.1.call-start = ((), (), s32[]{:S(2)}) async-start(), calls=%async_computation | async-start | bytes 1048576 | tf_op jit(solution)/shard_map/psum | solution.py:32
Sparse Core Ops, SparseCore 0:
  126.5 275.6 all-reduce.9
  603.9 274.2 all-reduce.7
where the time goes:
time: 982 us; the launch traced here: 971 us
  waiting for transfers between devices  550 us (56%)
  blocking collectives  381 us (39%)
  other arithmetic  23.8 us (2%)
  between operations  14.8 us (2%)
    psum x2, waiting for transfers between devices, on_device(): site_num, site_den = lax.psum((site_num, site_den), 'ev')  550 us
    psum x2, blocking collectives, on_device(): absum, count = lax.psum((abs_part, count_part), ('ev', 'ch'))  215 us
    psum x2, blocking collectives, on_device(): lax.psum((jnp.sum(product, axis=2), jnp.sum(weight, axis=2)), 'ch')  166 us
  transfers between devices with their start and end apart: 2, of which 2 were waited for; matrix products, arithmetic and copies ran while one was open for 0% of the time, Pallas kernels for 0%

commit v1 on v0

v1 whole, which is shorter than its diff:
```python
import functools
import jax
import jax.numpy as jnp
from jax import lax
from jax.experimental import pallas as pl
from jax.experimental.pallas import tpu as pltpu
from jax.sharding import PartitionSpec as P

ITERS = 2
LANES = 128
X, Y_LO, CORE, Y_HI, Z = 4, 4, 2, 2, 8
Y = Y_HI * Y_LO
CHIPS = X * Y_LO
f32 = jnp.float32


def ring(step, size):
    return min(step, size - step)


STAGE_A = sorted(
    ((dz, dc) for dz in range(Z) for dc in range(CORE) if dz or dc),
    key=lambda s: -ring(s[0], Z),
)
STAGE_B = sorted(
    ((dy, dx) for dy in range(Y) for dx in range(X) if dy or dx),
    key=lambda s: -ring(s[0], Y) - ring(s[1], X),
)
GROUP = sorted(
    ((dx, dy) for dx in range(X) for dy in range(Y_LO) if dx or dy),
    key=lambda s: -ring(s[0], X) - (0, 1.5, 2, 1.5)[s[1]],
)
CHAN = sorted(
    ((dh, dz) for dh in range(Y_HI) for dz in range(Z) if dh or dz),
    key=lambda s: -4 * s[0] - ring(s[1], Z),
)


def kernel(
    spectra, mask_h, source_h, site_h, event_h, channel_h, atten_h,
    source_o, site_o,
    rbuf, site, chan, srcv, attv, maskv, mask, evp, chx, srcb, dsb, sn, sd,
    away, recv_s, own, recv_c, gath, bsend, brecv, arow, arecv_a, arecv_b,
    spec_sem, in_sem, s_send, s_recv, c_send, c_recv, g_send, g_recv, f_send, f_recv,
    b_send, b_recv, aa_send, aa_recv, ab_send, ab_recv,
):
    n_ev, freqs, n_ch = rbuf.shape
    tiles = n_ch // LANES
    half = tiles // 2
    ev, ch = lax.axis_index("ev"), lax.axis_index("ch")
    core, chip = lax.rem(ev, CORE), ev // CORE
    x, y_lo = chip // Y_LO, lax.rem(chip, Y_LO)
    y_hi, z = ch // Z, lax.rem(ch, Z)
    y = y_hi * Y_LO + y_lo

    def place(px, py, pz, pc):
        return ((px * Y_LO + lax.rem(py, Y_LO)) * CORE + pc, (py // Y_LO) * Z + pz)

    stage_a = [place(x, y, lax.rem(z + dz, Z), lax.rem(core + dc, CORE)) for dz, dc in STAGE_A]
    stage_b = [place(lax.rem(x + dx, X), lax.rem(y + dy, Y), z, core) for dy, dx in STAGE_B]
    group_chip = [lax.rem(x + dx, X) * Y_LO + lax.rem(y_lo + dy, Y_LO) for dx, dy in GROUP]
    group_from = [lax.rem(x + X - dx, X) * Y_LO + lax.rem(y_lo + Y_LO - dy, Y_LO) for dx, dy in GROUP]
    group = [(g * CORE + core, ch) for g in group_chip]
    sibling = (chip * CORE + 1 - core, ch)
    chan_peers = [(ev, lax.rem(y_hi + dh, Y_HI) * Z + lax.rem(z + dz, Z)) for dh, dz in CHAN]

    def remote(src, dst, send, recv, peer):
        return pltpu.make_async_remote_copy(
            src_ref=src, dst_ref=dst, send_sem=send, recv_sem=recv,
            device_id=peer, device_id_type=pl.DeviceIdType.MESH,
        )

    def spec_copy(e):
        return pltpu.make_async_copy(spectra.at[e], rbuf.at[e], spec_sem.at[e])

    small = [
        pltpu.make_async_copy(src, dst, in_sem.at[i])
        for i, (src, dst) in enumerate(
            [(mask_h, mask), (event_h, evp), (channel_h, chan), (atten_h, attv),
             (source_h, srcv), (mask_h, maskv), (site_h, site)]
        )
    ]
    for copy in small:
        copy.start()

    @pl.loop(0, n_ev)
    def _(e):
        spec_copy(e).start()

    barrier = pltpu.get_barrier_semaphore()
    for peer in stage_a + stage_b:
        pl.semaphore_signal(barrier, inc=1, device_id=peer, device_id_type=pl.DeviceIdType.MESH)

    shape = (freqs, LANES)
    rows = lax.broadcasted_iota(jnp.int32, shape, 0)
    lanes = lax.broadcasted_iota(jnp.int32, shape, 1)
    diag = rows == lanes

    def to_column(row):
        spread = jnp.where(diag, jnp.broadcast_to(row, shape), 0.0)
        return jnp.sum(spread, axis=1, keepdims=True)

    def to_row(column):
        spread = jnp.where(diag, jnp.broadcast_to(column, shape), 0.0)
        return jnp.sum(spread, axis=0, keepdims=True)

    pending = []

    def all_sum(phase, row):
        arow[phase, 0] = row
        for stage, peers, landed, send, recv in (
            (0, stage_a, arecv_a, aa_send, aa_recv),
            (1, stage_b, arecv_b, ab_send, ab_recv),
        ):
            copies = [
                remote(arow.at[phase, stage], landed.at[phase, k], send.at[phase, k], recv.at[phase, k], peer)
                for k, peer in enumerate(peers)
            ]
            for copy in copies:
                copy.start()
            total = row
            for k, copy in enumerate(copies):
                copy.wait_recv()
            parts = [row] + [landed[phase, k] for k in range(len(peers))]
            while len(parts) > 1:
                parts = [a + b for a, b in zip(parts[::2], parts[1::2])] + parts[len(parts) // 2 * 2:]
            row = parts[0]
            if stage == 0:
                arow[phase, 1] = row
            pending.extend(copies)
        return row

    for copy in small:
        copy.wait()

    small_shape = (n_ev, freqs)
    small_diag = lax.broadcasted_iota(jnp.int32, small_shape, 0) == lax.broadcasted_iota(jnp.int32, small_shape, 1)

    def widen(row):
        spread = jnp.where(small_diag, jnp.broadcast_to(row, small_shape), 0.0)
        return jnp.broadcast_to(jnp.sum(spread, axis=1, keepdims=True), shape)

    for t in range(tiles):
        chx[0, t:t + 1, :] = chan[0:1, t * LANES:(t + 1) * LANES]
        chx[1, t:t + 1, :] = chan[1:2, t * LANES:(t + 1) * LANES]
    for e in range(n_ev):
        srcb[e] = widen(srcv[e:e + 1, :])
    attb = widen(attv[0:1, :])
    count = float(LANES) * jnp.sum(maskv[...].astype(f32), keepdims=True)

    zero = jnp.zeros(shape, f32)
    for it in range(ITERS):
        def magnitudes(e, carry, it=it):
            accs = list(carry)
            if it == 0:
                spec_copy(e).wait()
                east = evp[0, e] - chx[0]
                north = evp[1, e] - chx[1]
                travel = jnp.sqrt(east * east + north * north + evp[2, e] * evp[2, e]) * (1.0 / 3.0)
                level = srcb[e]
            else:
                level = dsb[e]
            for t in range(tiles):
                at = slice(t * LANES, (t + 1) * LANES)
                if it == 0:
                    r = rbuf[e, :, at] - level - site[:, at] + attb * jnp.broadcast_to(travel[t:t + 1, :], shape)
                else:
                    r = rbuf[e, :, at] - level - gath[it - 1, t]
                rbuf[e, :, at] = r
                accs[t % 2] = accs[t % 2] + jnp.abs(r) * mask[e, t].astype(f32)
            return tuple(accs)

        acc = lax.fori_loop(0, n_ev, magnitudes, (zero, zero))
        row = to_row(jnp.sum(acc[0] + acc[1], axis=1, keepdims=True))
        row = jnp.where(lanes[0:1] == freqs, count, row)
        if it == 0:
            pl.semaphore_wait(barrier, len(stage_a) + len(stage_b))
        total = all_sum(it, row)
        number = jnp.sum(jnp.where(lanes[0:1] == freqs, total, 0.0), axis=1, keepdims=True)
        mean = to_column(total) / jnp.maximum(jnp.broadcast_to(number, (freqs, 1)), 1.0)
        limit = jnp.broadcast_to(1.345 * (1.2533 * mean + 1e-05), shape)

        for e in range(n_ev):
            sn[e] = zero
            sd[e] = zero

        def weigh(first, into):
            def pair(j, carry):
                sums = [zero] * 4
                for e in range(n_ev):
                    num = den = None
                    for u in range(2):
                        t = first + 2 * j + u
                        r = rbuf[e, :, pl.ds(pl.multiple_of(t * LANES, LANES), LANES)]
                        w = limit * mask[e, t].astype(f32) / jnp.maximum(jnp.abs(r), limit)
                        p = w * r
                        sums[2 * u] += p
                        sums[2 * u + 1] += w
                        num = p if num is None else num + p
                        den = w if den is None else den + w
                    sn[e] += num
                    sd[e] += den
                for u in range(2):
                    into[2 * j + u, 0] = sums[2 * u]
                    into[2 * j + u, 1] = sums[2 * u + 1]
                return carry
            return pair

        to_sibling = remote(away.at[it], recv_s.at[it], s_send.at[it], s_recv.at[it], sibling)
        lax.fori_loop(0, half // 2, weigh((1 - core) * half, away.at[it]), 0)
        to_sibling.start()
        pending.append(to_sibling)
        lax.fori_loop(0, half // 2, weigh(core * half, own.at[it]), 0)
        to_sibling.wait_recv()
        scatter = []
        for k, g in enumerate(group_chip):
            own[it, g] += recv_s[it, g]
            copy = remote(own.at[it, g], recv_c.at[it, k], c_send.at[it, k], c_recv.at[it, k], group[k])
            copy.start()
            scatter.append(copy)
        pending.extend(scatter)

        packed = zero
        for e in range(n_ev):
            packed = jnp.where(lanes == e, jnp.sum(sn[e], axis=1, keepdims=True), packed)
            packed = jnp.where(lanes == n_ev + e, jnp.sum(sd[e], axis=1, keepdims=True), packed)
        packed = packed[0:8] + pltpu.roll(packed[8:16], 2 * n_ev, axis=1)
        bsend[it] = packed
        along = [
            remote(bsend.at[it], brecv.at[it, k], b_send.at[it, k], b_recv.at[it, k], peer)
            for k, peer in enumerate(chan_peers)
        ]
        for copy in along:
            copy.start()
        pending.extend(along)

        for copy in scatter:
            copy.wait_recv()
        both = own[it, chip] + recv_s[it, chip]
        for k in range(len(group)):
            both = both + recv_c[it, k]
        tile = core * half + chip
        gath[it, tile] = 0.5 * both[0] / (both[1] + 1.0)
        gather = [
            remote(gath.at[it, tile], gath.at[it, tile], g_send.at[it, k], g_recv.at[it, k], peer)
            for k, peer in enumerate(group)
        ]
        if it == ITERS - 1:
            final = site[:, pl.ds(pl.multiple_of(tile * LANES, LANES), LANES)]
            for i in range(ITERS):
                final = final + gath[i, tile]
            last_row = to_row(jnp.sum(final, axis=1, keepdims=True))
        for copy in gather:
            copy.start()
        pending.extend(gather)
        forward = [remote(gath.at[it, tile], gath.at[it, tile], f_send.at[it, 15], f_recv.at[it, 15], sibling)]
        forward[0].start()

        def gather_rest():
            for k, g in enumerate(group_from):
                gather[k].wait_recv()
                come = core * half + g
                copy = remote(gath.at[it, come], gath.at[it, come], f_send.at[it, k], f_recv.at[it, k], sibling)
                copy.start()
                forward.append(copy)
            pending.extend(forward)

        def source_rest():
            for copy in along:
                copy.wait_recv()
            both = bsend[it]
            for k in range(len(chan_peers)):
                both = both + brecv[it, k]
            use = lax.rem(lanes[0:8], 2 * n_ev) < n_ev
            below = jnp.where(use, pltpu.roll(both, LANES - n_ev, axis=1), 0.0)
            step = 0.5 * both / (below + 1.0)
            for e in range(n_ev):
                dsb[e, 0:8] = jnp.broadcast_to(step[:, e:e + 1], (8, LANES))
                dsb[e, 8:16] = jnp.broadcast_to(step[:, 2 * n_ev + e:2 * n_ev + e + 1], (8, LANES))
                srcb[e] += dsb[e]

        if it < ITERS - 1:
            gather_rest()
            source_rest()
            for copy in forward:
                copy.wait_recv()
        else:
            total = all_sum(ITERS, last_row) * (1.0 / (n_ch * Y_HI * Z))
            gather_rest()
            source_rest()
            for copy in forward:
                copy.wait_recv()

    shift = jnp.broadcast_to(to_column(total), shape)
    for t in range(tiles):
        at = slice(t * LANES, (t + 1) * LANES)
        out = site[:, at]
        for i in range(ITERS):
            out = out + gath[i, t]
        site_o[:, at] = out - shift
    for e in range(n_ev):
        out = to_row(srcb[e][:, 0:1]) + total
        source_o[e:e + 1, :] = out[:, 0:freqs]
    for copy in pending:
        copy.wait_send()


def on_device(spectra, tile_mask, source_init, site_init, event_pos, channel_pos, atten):
    n_ev, freqs, n_ch = spectra.shape
    tiles = n_ch // LANES
    half = tiles // 2
    assert half == CHIPS and freqs == n_ev == 16
    v, dma = pltpu.VMEM, pltpu.SemaphoreType.DMA
    ng, na, nb, nc = len(GROUP), len(STAGE_A), len(STAGE_B), len(CHAN)
    block = (freqs, LANES)
    scratch = [
        v((n_ev, freqs, n_ch), f32), v((freqs, n_ch), f32), v((2, n_ch), f32), v((n_ev, freqs), f32),
        v((1, freqs), f32), v((n_ev, tiles), jnp.int32),
        pltpu.SMEM((n_ev, tiles), jnp.int32), pltpu.SMEM((3, n_ev), f32),
        v((2, tiles, LANES), f32), v((n_ev,) + block, f32), v((n_ev,) + block, f32),
        v((n_ev,) + block, f32), v((n_ev,) + block, f32),
        v((ITERS, half, 2) + block, f32), v((ITERS, half, 2) + block, f32), v((ITERS, half, 2) + block, f32),
        v((ITERS, ng, 2) + block, f32), v((ITERS, tiles) + block, f32),
        v((ITERS, 8, LANES), f32), v((ITERS, nc, 8, LANES), f32),
        v((ITERS + 1, 2, 1, LANES), f32), v((ITERS + 1, na, 1, LANES), f32), v((ITERS + 1, nb, 1, LANES), f32),
        dma((n_ev,)), dma((7,)), dma((ITERS,)), dma((ITERS,)),
        dma((ITERS, ng)), dma((ITERS, ng)), dma((ITERS, ng)), dma((ITERS, ng)),
        dma((ITERS, ng + 1)), dma((ITERS, ng + 1)), dma((ITERS, nc)), dma((ITERS, nc)),
        dma((ITERS + 1, na)), dma((ITERS + 1, na)), dma((ITERS + 1, nb)), dma((ITERS + 1, nb)),
    ]
    anywhere = pl.BlockSpec(memory_space=pl.ANY)
    vmem = pl.BlockSpec(memory_space=pltpu.VMEM)
    return pl.pallas_call(
        kernel,
        out_shape=(
            jax.ShapeDtypeStruct((n_ev, freqs), f32),
            jax.ShapeDtypeStruct((freqs, n_ch), f32),
        ),
        in_specs=[anywhere] * 7,
        out_specs=(vmem, vmem),
        scratch_shapes=scratch,
        name="estimate",
        compiler_params=pltpu.CompilerParams(
            collective_id=0, has_side_effects=True, vmem_limit_bytes=40 << 20
        ),
    )(spectra, tile_mask, source_init, site_init, event_pos, channel_pos, atten.reshape(1, freqs))


def solution(mesh):
    in_specs = (
        P("ev", None, "ch"),
        P("ev", "ch"),
        P("ev", None),
        P(None, "ch"),
        P(None, "ev"),
        P(None, "ch"),
        P(),
    )
    out_specs = (P("ev", None), P(None, "ch"))
    return jax.shard_map(
        on_device, mesh=mesh, in_specs=in_specs, out_specs=out_specs, check_vma=False
    )
```

time: 982 us -> 91.9 us (0.09); the launches traced: 971 us -> 91.5 us
  waiting for transfers between devices: 550 us -> 0 us
  blocking collectives: 381 us -> 0 us
  Pallas kernels: 0 us -> 82.9 us
  other arithmetic: 23.8 us -> 0 us
  between operations: 14.8 us -> 0.66 us
    psum x2 -> x0, waiting for transfers between devices: 550 us -> none  [on_device(): site_num, site_den = lax.psum((site_num, site_den), 'ev')]
    psum x4 -> x0, blocking collectives: 381 us -> none  [the longest x2 215 us: on_device(): absum, count = lax.psum((abs_part, count_part), ('ev', 'ch'))]
    pallas_call x0 -> x1, Pallas kernels: none -> 82.9 us  [on_device(): pl.pallas_call(kernel, out_shape=(jax.ShapeDtypeStruct((n_ev, freqs), f32...]
    reduce_sum x7 -> x0, other arithmetic: 20.6 us -> none  [the longest x2 10.7 us: on_device(): site_num = jnp.sum(product, axis=0)]
  transfers between devices with their start and end apart: 2 -> 0, of which waited for: 2 -> 0; matrix products, arithmetic and copies ran while one was open for 0% -> 0% of each run, Pallas kernels for 0% -> 0%
where the time goes in v1:
time: 91.9 us; the launch traced here: 91.5 us
  Pallas kernels  82.9 us (90%)
  local copies, waits for them, and re-layouts  7.92 us (9%)
    pallas_call x1, Pallas kernels, on_device(): pl.pallas_call(kernel, out_shape=(jax.ShapeDtypeStruct((n_ev, freqs), f32...  82.9 us
    unnamed x16, local copies, waits for them, and re-layouts  7.92 us

profile of v1, /device:TPU:1, one launch (start us, length us, event | category | flops | bytes accessed | tf_op | source)
XLA Modules:
  0.0 91.5 jit_solution(14508789614747554786)
XLA Ops:
  0.6 0.0 copy-start
  0.6 2.2 %copy-done = f32[16,16,4096]{2,1,0:T(8,128)S(1)} copy-done((f32[16,16,4096]{2,1,0:T(8,128)S(1)}, f32[16,16,4096]{2,1,0:T(8,128)}, u32[]{:S(2)}) %copy-start) | copy-done | bytes 4194328
  2.8 0.0 copy-start.1
  2.8 0.9 %copy-done.1 = f32[16,4096]{1,0:T(8,128)S(1)} copy-done((f32[16,4096]{1,0:T(8,128)S(1)}, f32[16,4096]{1,0:T(8,128)}, u32[]{:S(2)}) %copy-start.1) | copy-done | bytes 262168
  3.8 0.0 copy-start.2
  3.8 0.8 copy-done.2
  4.5 0.0 copy-start.3
  4.5 0.7 copy-done.3
  5.2 0.0 copy-start.4
  5.2 0.7 copy-done.4
  5.9 0.0 copy-start.5
  5.9 0.7 copy-done.5
  6.6 0.0 copy-start.6
  6.6 0.7 copy-done.6
  7.3 82.9 %estimate.1 = (f32[16,16]{1,0:T(8,128)S(1)}, f32[16,4096]{1,0:T(8,128)S(1)}) custom-call(f32[16,16,4096]{2,1,0:T(8,128)S(1)} %copy-done, s32[16,32]{1,0:T(8,128)S(1)} %copy-done.3, f32[16,16]{1,0:T(8,128)S(1)} %copy-done.4, f32[16,4096]{1,0:T(8,128)S(1)} %copy-done.1, f32[3,16]{1,0:T(4,128)S(1)} %copy-done.5, f32[2,4096]{1,0:T(2,128)S(1)} %copy-done.2, ...), custom_call_target="tpu_custom_call" | custom-call | tf_op jit(solution)/shard_map/estimate/pallas_call | solution.py:333
  90.2 0.6 copy.11
  90.8 0.7 copy.12
Async XLA Ops:
  0.6 2.2 %copy-start = (f32[16,16,4096]{2,1,0:T(8,128)S(1)}, f32[16,16,4096]{2,1,0:T(8,128)}, u32[]{:S(2)}) copy-start(f32[16,16,4096]{2,1,0:T(8,128)} %spectra.1) | copy-start | bytes 12582916
  2.8 0.9 %copy-start.1 = (f32[16,4096]{1,0:T(8,128)S(1)}, f32[16,4096]{1,0:T(8,128)}, u32[]{:S(2)}) copy-start(f32[16,4096]{1,0:T(8,128)} %site_h.1) | copy-start | bytes 786436
  3.8 0.8 copy-start.2
  4.5 0.7 copy-start.3
  5.2 0.7 copy-start.4
  5.9 0.7 copy-start.5
  6.6 0.7 copy-start.6

commit v2 on v1

v2 whole, which is shorter than its diff:
```python
import functools
import jax
import jax.numpy as jnp
from jax import lax
from jax.experimental import pallas as pl
from jax.experimental.pallas import tpu as pltpu
from jax.sharding import PartitionSpec as P

ITERS = 2
LANES = 128
X, Y_LO, CORE, Y_HI, Z = 4, 4, 2, 2, 8
Y = Y_HI * Y_LO
CHIPS = X * Y_LO
f32 = jnp.float32


def ring(step, size):
    return min(step, size - step)


STAGE_A = sorted(
    ((dz, dc) for dz in range(Z) for dc in range(CORE) if dz or dc),
    key=lambda s: -ring(s[0], Z),
)
STAGE_B = sorted(
    ((dy, dx) for dy in range(Y) for dx in range(X) if dy or dx),
    key=lambda s: -ring(s[0], Y) - ring(s[1], X),
)
NEAR = 8


def group_step(p):
    i = p // X
    return (p % X + 1) % X, (2 + i + i * (i - 1) // 2) % Y_LO


def kernel(
    spectra, mask_h, source_h, site_h, event_h, channel_h, atten_h,
    source_o, site_o,
    rbuf, site, chan, srcv, attv, maskv, mask, evp, chx, srcb, dsb, sn, sd, sums,
    away, recv_s, own, recv_x, ysend, recv_y, gath, bsend, brecv, brecv2, arow, arecv_a, arecv_b,
    spec_sem, in_sem, s_send, s_recv, x_send, x_recv, y_send, y_recv, g_send, g_recv, f_send, f_recv,
    b_send, b_recv, a_send, a_recv,
):
    n_ev, freqs, n_ch = rbuf.shape
    tiles = n_ch // LANES
    half = tiles // 2
    part = n_ev // 4
    others = half - 1
    ev, ch = lax.axis_index("ev"), lax.axis_index("ch")
    core, chip = lax.rem(ev, CORE), ev // CORE
    x, y_lo = chip // Y_LO, lax.rem(chip, Y_LO)
    y_hi, z = ch // Z, lax.rem(ch, Z)
    y = y_hi * Y_LO + y_lo

    def place(px, py, pz, pc):
        return ((px * Y_LO + lax.rem(py, Y_LO)) * CORE + pc, (py // Y_LO) * Z + pz)

    stage_a = [place(x, y, lax.rem(z + dz, Z), lax.rem(core + dc, CORE)) for dz, dc in STAGE_A]
    stage_b = [place(lax.rem(x + dx, X), lax.rem(y + dy, Y), z, core) for dy, dx in STAGE_B]
    sibling = (chip * CORE + 1 - core, ch)
    along_z = [(ev, y_hi * Z + lax.rem(z + dz, Z)) for dz in (4, 3, 5, 2, 6, 1, 7)]
    across_y = (ev, (1 - y_hi) * Z + z)

    upper, inner = y_lo // 2, lax.rem((y_lo + 1) // 2, 2)

    def row_of(i):
        there = (1 - upper) * (Y_LO - 1 - i) + upper * i
        return there + i // 2 * inner * (1 - 2 * lax.rem(there, 2))

    across_x = [lax.rem(x + j + 1, X) * Y_LO for j in range(X)]

    def chip_at(p):
        dx, dy = group_step(p)
        return lax.rem(x + dx, X) * Y_LO + lax.rem(y_lo + dy, Y_LO)

    def chip_from(p):
        dx, dy = group_step(p)
        return lax.rem(x + X - dx, X) * Y_LO + lax.rem(y_lo + Y_LO - dy, Y_LO)

    barrier = pltpu.get_barrier_semaphore()
    for peer in stage_b + stage_a:
        pl.semaphore_signal(barrier, inc=1, device_id=peer, device_id_type=pl.DeviceIdType.MESH)

    def remote(src, dst, send, recv, peer):
        return pltpu.make_async_remote_copy(
            src_ref=src, dst_ref=dst, send_sem=send, recv_sem=recv,
            device_id=peer, device_id_type=pl.DeviceIdType.MESH,
        )

    def settle(ref, sem):
        pltpu.make_async_copy(ref, ref, sem).wait()

    def spec_copy(q):
        return pltpu.make_async_copy(spectra.at[pl.ds(q * part, part)], rbuf.at[pl.ds(q * part, part)], spec_sem.at[q])

    small = [
        pltpu.make_async_copy(src, dst, in_sem.at[i])
        for i, (src, dst) in enumerate(
            [(mask_h, mask), (event_h, evp), (channel_h, chan), (atten_h, attv),
             (source_h, srcv), (mask_h, maskv), (site_h, site)]
        )
    ]
    for copy in small:
        copy.start()
    for q in range(n_ev // part):
        spec_copy(q).start()

    shape = (freqs, LANES)
    rows = lax.broadcasted_iota(jnp.int32, shape, 0)
    lanes = lax.broadcasted_iota(jnp.int32, shape, 1)
    diag = rows == lanes

    def to_column(row):
        spread = jnp.where(diag, jnp.broadcast_to(row, shape), 0.0)
        return jnp.sum(spread, axis=1, keepdims=True)

    def to_row(column):
        spread = jnp.where(diag, jnp.broadcast_to(column, shape), 0.0)
        return jnp.sum(spread, axis=0, keepdims=True)

    def tree(parts):
        while len(parts) > 1:
            parts = [a + b for a, b in zip(parts[::2], parts[1::2])] + parts[len(parts) // 2 * 2:]
        return parts[0]

    sent = []

    def all_sum(phase, row, meanwhile=None):
        for stage, peers, landed in ((0, stage_a, arecv_a), (1, stage_b, arecv_b)):
            arow[phase, stage] = row
            for k, peer in enumerate(peers):
                remote(arow.at[phase, stage], landed.at[phase, k], a_send.at[phase, stage], a_recv.at[phase, stage], peer).start()
            sent.append((landed.at[phase], a_send.at[phase, stage]))
            if meanwhile is not None:
                meanwhile[stage]()
            settle(landed.at[phase], a_recv.at[phase, stage])
            row = tree([row] + [landed[phase, k] for k in range(len(peers))])
        return row

    for copy in small[:-1]:
        copy.wait()

    small_shape = (n_ev, freqs)
    small_diag = lax.broadcasted_iota(jnp.int32, small_shape, 0) == lax.broadcasted_iota(jnp.int32, small_shape, 1)

    def widen(row):
        spread = jnp.where(small_diag, jnp.broadcast_to(row, small_shape), 0.0)
        return jnp.broadcast_to(jnp.sum(spread, axis=1, keepdims=True), shape)

    for t in range(tiles):
        chx[0, t:t + 1, :] = chan[0:1, t * LANES:(t + 1) * LANES]
        chx[1, t:t + 1, :] = chan[1:2, t * LANES:(t + 1) * LANES]
    for e in range(n_ev):
        srcb[e] = widen(srcv[e:e + 1, :])
    attb = widen(attv[0:1, :])
    count = float(LANES) * jnp.sum(maskv[...].astype(f32), keepdims=True)

    small[-1].wait()
    zero = jnp.zeros(shape, f32)
    for it in range(ITERS):
        def first(e, carry):
            accs = list(carry)

            @pl.when(lax.rem(e, part) == 0)
            def _():
                spec_copy(e // part).wait()
            east = evp[0, e] - chx[0]
            north = evp[1, e] - chx[1]
            travel = jnp.sqrt(east * east + north * north + evp[2, e] * evp[2, e]) * (1.0 / 3.0)
            for t in range(tiles):
                at = slice(t * LANES, (t + 1) * LANES)
                r = rbuf[e, :, at] - srcb[e] - site[:, at] + attb * jnp.broadcast_to(travel[t:t + 1, :], shape)
                rbuf[e, :, at] = r
                accs[t % 2] = accs[t % 2] + jnp.abs(r) * mask[e, t].astype(f32)
            return tuple(accs)

        def later(side, it=it):
            def update(e, carry):
                accs = list(carry)
                for t in range(side * half, (side + 1) * half):
                    at = slice(t * LANES, (t + 1) * LANES)
                    r = rbuf[e, :, at] - dsb[e] - gath[it - 1, t]
                    rbuf[e, :, at] = r
                    accs[t % 2] = accs[t % 2] + jnp.abs(r) * mask[e, t].astype(f32)
                return tuple(accs)
            return update

        if it == 0:
            first_sum, second_sum = lax.fori_loop(0, n_ev, first, (zero, zero))
            sums[...] = first_sum + second_sum
        else:
            for side in range(CORE):
                @pl.when(core == side)
                def _(side=side, it=it):
                    acc = lax.fori_loop(0, n_ev, later(side), (zero, zero))
                    settle(gath.at[it - 1, pl.ds(0, half)], f_recv.at[it - 1])
                    acc = lax.fori_loop(0, n_ev, later(1 - side), acc)
                    sums[...] = acc[0] + acc[1]
        row = to_row(jnp.sum(sums[...], axis=1, keepdims=True))
        row = jnp.where(lanes[0:1] == freqs, count, row)
        if it == 0:
            pl.semaphore_wait(barrier, len(stage_a) + len(stage_b))
        total = all_sum(it, row)
        number = jnp.sum(jnp.where(lanes[0:1] == freqs, total, 0.0), axis=1, keepdims=True)
        mean = to_column(total) / jnp.maximum(jnp.broadcast_to(number, (freqs, 1)), 1.0)
        limit = jnp.broadcast_to(1.345 * (1.2533 * mean + 1e-05), shape)

        for e in range(n_ev):
            sn[e] = zero
            sd[e] = zero

        def weigh(side, into, i):
            row = row_of(i)
            for j in range(0, X, 2):
                totals = [zero] * 4
                where = [side * half + across_x[j + u] + row for u in range(2)]
                for e in range(n_ev):
                    num = den = None
                    for u, t in enumerate(where):
                        r = rbuf[e, :, pl.ds(pl.multiple_of(t * LANES, LANES), LANES)]
                        w = limit * mask[e, t].astype(f32) / jnp.maximum(jnp.abs(r), limit)
                        p = w * r
                        totals[2 * u] += p
                        totals[2 * u + 1] += w
                        num = p if num is None else num + p
                        den = w if den is None else den + w
                    sn[e] += num
                    sd[e] += den
                for u in range(2):
                    into[X * i + j + u, 0] = totals[2 * u]
                    into[X * i + j + u, 1] = totals[2 * u + 1]

        def give(i, carry):
            weigh(1 - core, away.at[it], i)
            block = pl.ds(X * i, X)
            remote(away.at[it, block], recv_s.at[it, block], s_send.at[it], s_recv.at[it, i], sibling).start()
            return carry

        def take(i, carry):
            weigh(core, own.at[it], i)
            settle(recv_s.at[it, pl.ds(X * i, X)], s_recv.at[it, i])
            for j in (1, 0, 2, 3):
                p = X * i + j
                own[it, p] += recv_s[it, p]
                if j < X - 1:
                    peer = (across_x[j] + y_lo) * CORE + core
                    remote(own.at[it, p], recv_x.at[it, i, j], x_send.at[it], x_recv.at[it, i], (peer, ch)).start()
            return carry

        lax.fori_loop(0, Y_LO, give, 0)
        lax.fori_loop(0, Y_LO, take, 0)
        sent.append((recv_s.at[it], s_send.at[it]))
        sent.append((recv_x.at[it], x_send.at[it]))

        packed = zero
        for e in range(n_ev):
            packed = jnp.where(lanes == e, jnp.sum(sn[e], axis=1, keepdims=True), packed)
            packed = jnp.where(lanes == n_ev + e, jnp.sum(sd[e], axis=1, keepdims=True), packed)
        packed = packed[0:8] + pltpu.roll(packed[8:16], 2 * n_ev, axis=1)
        bsend[it, 0] = packed
        for k, peer in enumerate(along_z):
            remote(bsend.at[it, 0], brecv.at[it, k], b_send.at[it, 0], b_recv.at[it, 0], peer).start()
        sent.append((brecv.at[it], b_send.at[it, 0]))

        for i in range(Y_LO):
            settle(recv_x.at[it, i], x_recv.at[it, i])
            both = tree([own[it, X * i + X - 1]] + [recv_x[it, i, j] for j in range(X - 1)])
            if i < Y_LO - 1:
                ysend[it, i] = both
                slot = lax.rem(row_of(i) + Y_LO - y_lo, Y_LO) - 1
                peer = (x * Y_LO + row_of(i)) * CORE + core
                remote(ysend.at[it, i], recv_y.at[it, slot], y_send.at[it], y_recv.at[it], (peer, ch)).start()
        sent.append((recv_y.at[it], y_send.at[it]))
        settle(recv_y.at[it], y_recv.at[it])
        both = tree([both] + [recv_y[it, i] for i in range(Y_LO - 1)])
        tile = core * half + chip
        gath[it, tile] = 0.5 * both[0] / (both[1] + 1.0)
        if it == ITERS - 1:
            final = site[:, pl.ds(pl.multiple_of(tile * LANES, LANES), LANES)]
            for i in range(ITERS):
                final = final + gath[i, tile]
            last_row = to_row(jnp.sum(final, axis=1, keepdims=True))

        def gather():
            for p in range(others):
                batch = 0 if p < NEAR else 1
                remote(
                    gath.at[it, tile], gath.at[it, tile], g_send.at[it, batch], g_recv.at[it, batch],
                    (chip_at(p) * CORE + core, ch),
                ).start()
            remote(gath.at[it, tile], gath.at[it, tile], f_send.at[it], f_recv.at[it], sibling).start()
            for batch, n in ((0, NEAR), (1, others - NEAR)):
                sent.append((gath.at[it, pl.ds(0, n)], g_send.at[it, batch]))
            sent.append((gath.at[it, pl.ds(0, half)], f_send.at[it]))

        def across():
            settle(brecv.at[it], b_recv.at[it, 0])
            bsend[it, 1] = tree([bsend[it, 0]] + [brecv[it, k] for k in range(len(along_z))])
            remote(bsend.at[it, 1], brecv2.at[it], b_send.at[it, 1], b_recv.at[it, 1], across_y).start()
            sent.append((brecv2.at[it], b_send.at[it, 1]))

        def source_rest():
            settle(brecv2.at[it], b_recv.at[it, 1])
            both = bsend[it, 1] + brecv2[it]
            use = lax.rem(lanes[0:8], 2 * n_ev) < n_ev
            below = jnp.where(use, pltpu.roll(both, LANES - n_ev, axis=1), 0.0)
            step = 0.5 * both / (below + 1.0)
            for e in range(n_ev):
                dsb[e, 0:8] = jnp.broadcast_to(step[:, e:e + 1], (8, LANES))
                dsb[e, 8:16] = jnp.broadcast_to(step[:, 2 * n_ev + e:2 * n_ev + e + 1], (8, LANES))
                srcb[e] += dsb[e]

        def forward():
            for batch, (first, last) in enumerate(((0, NEAR), (NEAR, others))):
                settle(gath.at[it, pl.ds(0, last - first)], g_recv.at[it, batch])
                for p in range(first, last):
                    come = core * half + chip_from(p)
                    remote(gath.at[it, come], gath.at[it, come], f_send.at[it], f_recv.at[it], sibling).start()

        if it < ITERS - 1:
            gather()
            across()
            forward()
            source_rest()
        else:
            def meanwhile():
                across()
                forward()
            total = all_sum(ITERS, last_row, (gather, meanwhile)) * (1.0 / (n_ch * Y_HI * Z))
            source_rest()
            settle(gath.at[it, pl.ds(0, half)], f_recv.at[it])

    shift = jnp.broadcast_to(to_column(total), shape)
    for t in range(tiles):
        at = slice(t * LANES, (t + 1) * LANES)
        out = site[:, at]
        for i in range(ITERS):
            out = out + gath[i, t]
        site_o[:, at] = out - shift
    for e in range(n_ev):
        out = to_row(srcb[e][:, 0:1]) + total
        source_o[e:e + 1, :] = out[:, 0:freqs]
    for ref, sem in sent:
        settle(ref, sem)


def on_device(spectra, tile_mask, source_init, site_init, event_pos, channel_pos, atten):
    n_ev, freqs, n_ch = spectra.shape
    tiles = n_ch // LANES
    half = tiles // 2
    assert half == CHIPS and freqs == n_ev == 16
    v, dma = pltpu.VMEM, pltpu.SemaphoreType.DMA
    na, nb = len(STAGE_A), len(STAGE_B)
    block = (freqs, LANES)
    scratch = [
        v((n_ev, freqs, n_ch), f32), v((freqs, n_ch), f32), v((2, n_ch), f32), v((n_ev, freqs), f32),
        v((1, freqs), f32), v((n_ev, tiles), jnp.int32),
        pltpu.SMEM((n_ev, tiles), jnp.int32), pltpu.SMEM((3, n_ev), f32),
        v((2, tiles, LANES), f32), v((n_ev,) + block, f32), v((n_ev,) + block, f32),
        v((n_ev,) + block, f32), v((n_ev,) + block, f32), v(block, f32),
        v((ITERS, half, 2) + block, f32), v((ITERS, half, 2) + block, f32), v((ITERS, half, 2) + block, f32),
        v((ITERS, Y_LO, X - 1, 2) + block, f32), v((ITERS, Y_LO - 1, 2) + block, f32), v((ITERS, Y_LO - 1, 2) + block, f32),
        v((ITERS, tiles) + block, f32),
        v((ITERS, 2, 8, LANES), f32), v((ITERS, Z - 1, 8, LANES), f32), v((ITERS, 8, LANES), f32),
        v((ITERS + 1, 2, 1, LANES), f32), v((ITERS + 1, na, 1, LANES), f32), v((ITERS + 1, nb, 1, LANES), f32),
        dma((4,)), dma((7,)), dma((ITERS,)), dma((ITERS, Y_LO)), dma((ITERS,)), dma((ITERS, Y_LO)), dma((ITERS,)), dma((ITERS,)),
        dma((ITERS, 2)), dma((ITERS, 2)), dma((ITERS,)), dma((ITERS,)),
        dma((ITERS, 2)), dma((ITERS, 2)), dma((ITERS + 1, 2)), dma((ITERS + 1, 2)),
    ]
    hbm = pl.BlockSpec(memory_space=pltpu.HBM)
    vmem = pl.BlockSpec(memory_space=pltpu.VMEM)
    shapes = (jax.ShapeDtypeStruct((n_ev, freqs), f32), jax.ShapeDtypeStruct((freqs, n_ch), f32))
    inputs = (spectra, tile_mask, source_init, site_init, event_pos, channel_pos, atten.reshape(1, freqs))
    return pl.pallas_call(
        kernel,
        out_shape=shapes,
        in_specs=[hbm] * len(inputs),
        out_specs=(vmem, vmem),
        scratch_shapes=scratch,
        name="estimate",
        compiler_params=pltpu.CompilerParams(
            collective_id=0, has_side_effects=True, vmem_limit_bytes=40 << 20
        ),
    )(*[pltpu.with_memory_space_constraint(v, pltpu.HBM) for v in inputs])


def solution(mesh):
    in_specs = (
        P("ev", None, "ch"),
        P("ev", "ch"),
        P("ev", None),
        P(None, "ch"),
        P(None, "ev"),
        P(None, "ch"),
        P(),
    )
    out_specs = (P("ev", None), P(None, "ch"))
    return jax.shard_map(
        on_device, mesh=mesh, in_specs=in_specs, out_specs=out_specs, check_vma=False
    )
```

time: 91.9 us -> 73.5 us (0.80)
  Pallas kernels: 82.9 us -> 71.4 us
  local copies, waits for them, and re-layouts: 7.92 us -> 1.3 us
    pallas_call x1, Pallas kernels: 82.9 us -> 71.4 us  [on_device(): pl.pallas_call(kernel, out_shape=shapes, in_specs=[hbm] * len(inputs), ou...]
    unnamed x16 -> x2, local copies, waits for them, and re-layouts: 7.92 us -> 1.3 us
where the time goes in v2:
time: 73.5 us; the launch traced here: 73.3 us
  Pallas kernels  71.4 us (97%)
  local copies, waits for them, and re-layouts  1.3 us (2%)
    pallas_call x1, Pallas kernels, on_device(): pl.pallas_call(kernel, out_shape=shapes, in_specs=[hbm] * len(inputs), ou...  71.4 us

profile of v2, /device:TPU:1, one launch (start us, length us, event | category | flops | bytes accessed | tf_op | source)
XLA Modules:
  0.0 73.3 jit_solution(15208493741263287391)
XLA Ops:
  0.6 71.4 %estimate.1 = (f32[16,16]{1,0:T(8,128)S(1)}, f32[16,4096]{1,0:T(8,128)S(1)}) custom-call(f32[16,16,4096]{2,1,0:T(8,128)} %spectra.1, s32[16,32]{1,0:T(8,128)} %mask_h.1, f32[16,16]{1,0:T(8,128)} %source_h.1, f32[16,4096]{1,0:T(8,128)} %site_h.1, f32[3,16]{1,0:T(4,128)} %event_h.1, f32[2,4096]{1,0:T(2,128)} %channel_h.1, f32[1,16]{1,0:T(1,128)} %bitcast.1), custom_call_target="tpu_custom_call" | custom-call | tf_op jit(solution)/shard_map/estimate/pallas_call | solution.py:375
  72.0 0.6 copy.11
  72.6 0.7 copy.12

commit v3 on v2

--- a/solution.py
+++ b/solution.py
@@ -26,6 +26,10 @@
     ((dy, dx) for dy in range(Y) for dx in range(X) if dy or dx),
     key=lambda s: -ring(s[0], Y) - ring(s[1], X),
 )
+EVERYONE = sorted(
+    ((dx, dy, dz) for dx in range(X) for dy in range(Y) for dz in range(Z) if dx or dy or dz),
+    key=lambda s: -ring(s[0], X) - ring(s[1], Y) - ring(s[2], Z),
+)
 NEAR = 8
 
 
@@ -38,9 +42,9 @@
     spectra, mask_h, source_h, site_h, event_h, channel_h, atten_h,
     source_o, site_o,
     rbuf, site, chan, srcv, attv, maskv, mask, evp, chx, srcb, dsb, sn, sd, sums,
-    away, recv_s, own, recv_x, ysend, recv_y, gath, bsend, brecv, brecv2, arow, arecv_a, arecv_b,
+    away, recv_s, own, recv_x, ysend, recv_y, gath, bsend, brecv, brecv2, arow, arecv_a, arecv_b, arecv_all,
     spec_sem, in_sem, s_send, s_recv, x_send, x_recv, y_send, y_recv, g_send, g_recv, f_send, f_recv,
-    b_send, b_recv, a_send, a_recv,
+    b_send, b_recv, a_send, a_recv, all_send, all_recv,
 ):
     n_ev, freqs, n_ch = rbuf.shape
     tiles = n_ch // LANES
@@ -126,17 +130,43 @@
 
     sent = []
 
-    def all_sum(phase, row, meanwhile=None):
+    def drain():
+        for ref, sem in sent:
+            settle(ref, sem)
+        sent.clear()
+
+    def all_sum(turn, row, after_first=None, after_second=None):
         for stage, peers, landed in ((0, stage_a, arecv_a), (1, stage_b, arecv_b)):
-            arow[phase, stage] = row
+            arow[turn, stage] = row
             for k, peer in enumerate(peers):
-                remote(arow.at[phase, stage], landed.at[phase, k], a_send.at[phase, stage], a_recv.at[phase, stage], peer).start()
-            sent.append((landed.at[phase], a_send.at[phase, stage]))
-            if meanwhile is not None:
-                meanwhile[stage]()
-            settle(landed.at[phase], a_recv.at[phase, stage])
-            row = tree([row] + [landed[phase, k] for k in range(len(peers))])
+                remote(arow.at[turn, stage], landed.at[turn, k], a_send.at[turn, stage], a_recv.at[turn, stage], peer).start()
+            sent.append((landed.at[turn], a_send.at[turn, stage]))
+            after = (after_first, after_second)[stage]
+            if after is not None:
+                after()
+            settle(landed.at[turn], a_recv.at[turn, stage])
+            row = tree([row] + [landed[turn, k] for k in range(len(peers))])
         return row
+
+    xs = [lax.rem(x + dx, X) for dx in range(X)]
+    ys = [lax.rem(y + dy, Y) for dy in range(Y)]
+    zs = [lax.rem(z + dz, Z) for dz in range(Z)]
+    ev_at = [[(px * Y_LO + lax.rem(py, Y_LO)) * CORE + core for py in ys] for px in xs]
+    ch_at = [[(py // Y_LO) * Z + pz for pz in zs] for py in ys]
+
+    def all_sum_direct(row):
+        arow[1, 0] = row
+        pair, landed = arecv_all.at[pl.ds(len(EVERYONE), 1)], arecv_all.at[pl.ds(0, len(EVERYONE))]
+        remote(arow.at[1, pl.ds(0, 1)], pair, all_send.at[0], all_recv.at[0], sibling).start()
+        settle(pair, all_recv.at[0])
+        row = row + arecv_all[len(EVERYONE)]
+        arow[1, 1] = row
+        for k, (dx, dy, dz) in enumerate(EVERYONE):
+            remote(arow.at[1, 1], arecv_all.at[k], all_send.at[1], all_recv.at[1], (ev_at[dx][dy], ch_at[dy][dz])).start()
+        sent.append((pair, all_send.at[0]))
+        sent.append((landed, all_send.at[1]))
+        settle(landed, all_recv.at[1])
+        return tree([row] + [arecv_all[k] for k in range(len(EVERYONE))])
 
     for copy in small[:-1]:
         copy.wait()
@@ -194,14 +224,15 @@
                 @pl.when(core == side)
                 def _(side=side, it=it):
                     acc = lax.fori_loop(0, n_ev, later(side), (zero, zero))
-                    settle(gath.at[it - 1, pl.ds(0, half)], f_recv.at[it - 1])
+                    settle(gath.at[it - 1, pl.ds(0, half)], f_recv.at[0])
                     acc = lax.fori_loop(0, n_ev, later(1 - side), acc)
                     sums[...] = acc[0] + acc[1]
         row = to_row(jnp.sum(sums[...], axis=1, keepdims=True))
         row = jnp.where(lanes[0:1] == freqs, count, row)
+        drain()
         if it == 0:
             pl.semaphore_wait(barrier, len(stage_a) + len(stage_b))
-        total = all_sum(it, row)
+        total = all_sum(0, row) if it == 0 else all_sum_direct(row)
         number = jnp.sum(jnp.where(lanes[0:1] == freqs, total, 0.0), axis=1, keepdims=True)
         mean = to_column(total) / jnp.maximum(jnp.broadcast_to(number, (freqs, 1)), 1.0)
         limit = jnp.broadcast_to(1.345 * (1.2533 * mean + 1e-05), shape)
@@ -234,24 +265,24 @@
         def give(i, carry):
             weigh(1 - core, away.at[it], i)
             block = pl.ds(X * i, X)
-            remote(away.at[it, block], recv_s.at[it, block], s_send.at[it], s_recv.at[it, i], sibling).start()
+            remote(away.at[it, block], recv_s.at[it, block], s_send.at[0], s_recv.at[i], sibling).start()
             return carry
 
         def take(i, carry):
             weigh(core, own.at[it], i)
-            settle(recv_s.at[it, pl.ds(X * i, X)], s_recv.at[it, i])
+            settle(recv_s.at[it, pl.ds(X * i, X)], s_recv.at[i])
             for j in (1, 0, 2, 3):
                 p = X * i + j
                 own[it, p] += recv_s[it, p]
                 if j < X - 1:
                     peer = (across_x[j] + y_lo) * CORE + core
-                    remote(own.at[it, p], recv_x.at[it, i, j], x_send.at[it], x_recv.at[it, i], (peer, ch)).start()
+                    remote(own.at[it, p], recv_x.at[it, i, j], x_send.at[0], x_recv.at[i], (peer, ch)).start()
             return carry
 
         lax.fori_loop(0, Y_LO, give, 0)
         lax.fori_loop(0, Y_LO, take, 0)
-        sent.append((recv_s.at[it], s_send.at[it]))
-        sent.append((recv_x.at[it], x_send.at[it]))
+        sent.append((recv_s.at[it], s_send.at[0]))
+        sent.append((recv_x.at[it], x_send.at[0]))
 
         packed = zero
         for e in range(n_ev):
@@ -260,19 +291,19 @@
         packed = packed[0:8] + pltpu.roll(packed[8:16], 2 * n_ev, axis=1)
         bsend[it, 0] = packed
         for k, peer in enumerate(along_z):
-            remote(bsend.at[it, 0], brecv.at[it, k], b_send.at[it, 0], b_recv.at[it, 0], peer).start()
-        sent.append((brecv.at[it], b_send.at[it, 0]))
+            remote(bsend.at[it, 0], brecv.at[it, k], b_send.at[0], b_recv.at[0], peer).start()
+        sent.append((brecv.at[it], b_send.at[0]))
 
         for i in range(Y_LO):
-            settle(recv_x.at[it, i], x_recv.at[it, i])
+            settle(recv_x.at[it, i], x_recv.at[i])
             both = tree([own[it, X * i + X - 1]] + [recv_x[it, i, j] for j in range(X - 1)])
             if i < Y_LO - 1:
                 ysend[it, i] = both
                 slot = lax.rem(row_of(i) + Y_LO - y_lo, Y_LO) - 1
                 peer = (x * Y_LO + row_of(i)) * CORE + core
-                remote(ysend.at[it, i], recv_y.at[it, slot], y_send.at[it], y_recv.at[it], (peer, ch)).start()
-        sent.append((recv_y.at[it], y_send.at[it]))
-        settle(recv_y.at[it], y_recv.at[it])
+                remote(ysend.at[it, i], recv_y.at[it, slot], y_send.at[0], y_recv.at[0], (peer, ch)).start()
+        sent.append((recv_y.at[it], y_send.at[0]))
+        settle(recv_y.at[it], y_recv.at[0])
         both = tree([both] + [recv_y[it, i] for i in range(Y_LO - 1)])
         tile = core * half + chip
         gath[it, tile] = 0.5 * both[0] / (both[1] + 1.0)
@@ -286,22 +317,21 @@
             for p in range(others):
                 batch = 0 if p < NEAR else 1
                 remote(
-                    gath.at[it, tile], gath.at[it, tile], g_send.at[it, batch], g_recv.at[it, batch],
+                    gath.at[it, tile], gath.at[it, tile], g_send.at[0], g_recv.at[batch],
                     (chip_at(p) * CORE + core, ch),
                 ).start()
-            remote(gath.at[it, tile], gath.at[it, tile], f_send.at[it], f_recv.at[it], sibling).start()
-            for batch, n in ((0, NEAR), (1, others - NEAR)):
-                sent.append((gath.at[it, pl.ds(0, n)], g_send.at[it, batch]))
-            sent.append((gath.at[it, pl.ds(0, half)], f_send.at[it]))
+            remote(gath.at[it, tile], gath.at[it, tile], f_send.at[0], f_recv.at[0], sibling).start()
+            sent.append((gath.at[it, pl.ds(0, others)], g_send.at[0]))
+            sent.append((gath.at[it, pl.ds(0, half)], f_send.at[0]))
 
         def across():
-            settle(brecv.at[it], b_recv.at[it, 0])
+            settle(brecv.at[it], b_recv.at[0])
             bsend[it, 1] = tree([bsend[it, 0]] + [brecv[it, k] for k in range(len(along_z))])
-            remote(bsend.at[it, 1], brecv2.at[it], b_send.at[it, 1], b_recv.at[it, 1], across_y).start()
-            sent.append((brecv2.at[it], b_send.at[it, 1]))
+            remote(bsend.at[it, 1], brecv2.at[it], b_send.at[1], b_recv.at[1], across_y).start()
+            sent.append((brecv2.at[it], b_send.at[1]))
 
         def source_rest():
-            settle(brecv2.at[it], b_recv.at[it, 1])
+            settle(brecv2.at[it], b_recv.at[1])
             both = bsend[it, 1] + brecv2[it]
             use = lax.rem(lanes[0:8], 2 * n_ev) < n_ev
             below = jnp.where(use, pltpu.roll(both, LANES - n_ev, axis=1), 0.0)
@@ -313,10 +343,10 @@
 
         def forward():
             for batch, (first, last) in enumerate(((0, NEAR), (NEAR, others))):
-                settle(gath.at[it, pl.ds(0, last - first)], g_recv.at[it, batch])
+                settle(gath.at[it, pl.ds(0, last - first)], g_recv.at[batch])
                 for p in range(first, last):
                     come = core * half + chip_from(p)
-                    remote(gath.at[it, come], gath.at[it, come], f_send.at[it], f_recv.at[it], sibling).start()
+                    remote(gath.at[it, come], gath.at[it, come], f_send.at[0], f_recv.at[0], sibling).start()
 
         if it < ITERS - 1:
             gather()
@@ -327,9 +357,9 @@
             def meanwhile():
                 across()
                 forward()
-            total = all_sum(ITERS, last_row, (gather, meanwhile)) * (1.0 / (n_ch * Y_HI * Z))
+            total = all_sum(2, last_row, gather, meanwhile) * (1.0 / (n_ch * Y_HI * Z))
             source_rest()
-            settle(gath.at[it, pl.ds(0, half)], f_recv.at[it])
+            settle(gath.at[it, pl.ds(0, half)], f_recv.at[0])
 
     shift = jnp.broadcast_to(to_column(total), shape)
     for t in range(tiles):
@@ -341,8 +371,17 @@
     for e in range(n_ev):
         out = to_row(srcb[e][:, 0:1]) + total
         source_o[e:e + 1, :] = out[:, 0:freqs]
-    for ref, sem in sent:
-        settle(ref, sem)
+    drain()
+
+
+def store(source, site, source_o, site_o, sem):
+    copies = [
+        pltpu.make_async_copy(src, dst, sem.at[i]) for i, (src, dst) in enumerate(((source, source_o), (site, site_o)))
+    ]
+    for copy in copies:
+        copy.start()
+    for copy in copies:
+        copy.wait()
 
 
 def on_device(spectra, tile_mask, source_init, site_init, event_pos, channel_pos, atten):
@@ -364,17 +403,17 @@
         v((ITERS, tiles) + block, f32),
         v((ITERS, 2, 8, LANES), f32), v((ITERS, Z - 1, 8, LANES), f32), v((ITERS, 8, LANES), f32),
         v((ITERS + 1, 2, 1, LANES), f32), v((ITERS + 1, na, 1, LANES), f32), v((ITERS + 1, nb, 1, LANES), f32),
-        dma((4,)), dma((7,)), dma((ITERS,)), dma((ITERS, Y_LO)), dma((ITERS,)), dma((ITERS, Y_LO)), dma((ITERS,)), dma((ITERS,)),
-        dma((ITERS, 2)), dma((ITERS, 2)), dma((ITERS,)), dma((ITERS,)),
-        dma((ITERS, 2)), dma((ITERS, 2)), dma((ITERS + 1, 2)), dma((ITERS + 1, 2)),
+        v((len(EVERYONE) + 1, 1, LANES), f32),
+        dma((4,)), dma((7,)), dma((1,)), dma((Y_LO,)), dma((1,)), dma((Y_LO,)), dma((1,)), dma((1,)),
+        dma((1,)), dma((2,)), dma((1,)), dma((1,)), dma((2,)), dma((2,)), dma((ITERS + 1, 2)), dma((ITERS + 1, 2)), dma((2,)), dma((2,)),
     ]
     hbm = pl.BlockSpec(memory_space=pltpu.HBM)
     vmem = pl.BlockSpec(memory_space=pltpu.VMEM)
     shapes = (jax.ShapeDtypeStruct((n_ev, freqs), f32), jax.ShapeDtypeStruct((freqs, n_ch), f32))
     inputs = (spectra, tile_mask, source_init, site_init, event_pos, channel_pos, atten.reshape(1, freqs))
-    return pl.pallas_call(
+    results = pl.pallas_call(
         kernel,
-        out_shape=shapes,
+        out_shape=tuple(pltpu.VMEM(v.shape, f32) for v in shapes),
         in_specs=[hbm] * len(inputs),
         out_specs=(vmem, vmem),
         scratch_shapes=scratch,
@@ -383,6 +422,14 @@
             collective_id=0, has_side_effects=True, vmem_limit_bytes=40 << 20
         ),
     )(*[pltpu.with_memory_space_constraint(v, pltpu.HBM) for v in inputs])
+    return pl.pallas_call(
+        store,
+        out_shape=shapes,
+        in_specs=[vmem, vmem],
+        out_specs=(hbm, hbm),
+        scratch_shapes=[dma((2,))],
+        name="store",
+    )(*[pltpu.with_memory_space_constraint(v, pltpu.VMEM) for v in results])
 
 
 def solution(mesh):

time: 73.5 us -> 72.9 us (level)
  local copies, waits for them, and re-layouts: 1.3 us -> 0 us
    unnamed x2 -> x0, local copies, waits for them, and re-layouts: 1.3 us -> none
    pallas_call x1 -> x2, Pallas kernels: 71.4 us -> 72.1 us  [the longest x1 71.4 us: on_device(): pl.pallas_call(kernel, out_shape=tuple((pltpu.VMEM(v.shape, f32) for v in...]
where the time goes in v3:
time: 72.9 us; the launch traced here: 72.8 us
  Pallas kernels  72.1 us (99%)
    pallas_call x1, Pallas kernels, on_device(): pl.pallas_call(kernel, out_shape=tuple((pltpu.VMEM(v.shape, f32) for v in...  71.4 us

profile of v3, /device:TPU:1, one launch (start us, length us, event | category | flops | bytes accessed | tf_op | source)
XLA Modules:
  0.0 72.8 jit_solution(13399487150970589128)
XLA Ops:
  0.6 71.4 %estimate.1 = (f32[16,16]{1,0:T(8,128)S(1)}, f32[16,4096]{1,0:T(8,128)S(1)}) custom-call(f32[16,16,4096]{2,1,0:T(8,128)} %spectra.1, s32[16,32]{1,0:T(8,128)} %mask_h.1, f32[16,16]{1,0:T(8,128)} %source_h.1, f32[16,4096]{1,0:T(8,128)} %site_h.1, f32[3,16]{1,0:T(4,128)} %event_h.1, f32[2,4096]{1,0:T(2,128)} %channel_h.1, f32[1,16]{1,0:T(1,128)} %bitcast.1), custom_call_target="tpu_custom_call" | custom-call | tf_op jit(solution)/shard_map/estimate/pallas_call | solution.py:414
  72.1 0.7 store.1

commit v4 on v3

--- a/solution.py
+++ b/solution.py
@@ -42,7 +42,7 @@
     spectra, mask_h, source_h, site_h, event_h, channel_h, atten_h,
     source_o, site_o,
     rbuf, site, chan, srcv, attv, maskv, mask, evp, chx, srcb, dsb, sn, sd, sums,
-    away, recv_s, own, recv_x, ysend, recv_y, gath, bsend, brecv, brecv2, arow, arecv_a, arecv_b, arecv_all,
+    away, recv_s, own, recv_x, ysend, recv_y, gath, bsend, brecv, brecv2, arow, arecv_p, arecv_a, arecv_b, arecv_all,
     spec_sem, in_sem, s_send, s_recv, x_send, x_recv, y_send, y_recv, g_send, g_recv, f_send, f_recv,
     b_send, b_recv, a_send, a_recv, all_send, all_recv,
 ):
@@ -83,7 +83,8 @@
         return lax.rem(x + X - dx, X) * Y_LO + lax.rem(y_lo + Y_LO - dy, Y_LO)
 
     barrier = pltpu.get_barrier_semaphore()
-    for peer in stage_b + stage_a:
+    greeted = stage_b + stage_a
+    for peer in greeted:
         pl.semaphore_signal(barrier, inc=1, device_id=peer, device_id_type=pl.DeviceIdType.MESH)
 
     def remote(src, dst, send, recv, peer):
@@ -135,17 +136,16 @@
             settle(ref, sem)
         sent.clear()
 
-    def all_sum(turn, row, after_first=None, after_second=None):
-        for stage, peers, landed in ((0, stage_a, arecv_a), (1, stage_b, arecv_b)):
+    def all_sum(turn, stages, row):
+        for stage, (peers, landed, after) in enumerate(stages):
             arow[turn, stage] = row
             for k, peer in enumerate(peers):
-                remote(arow.at[turn, stage], landed.at[turn, k], a_send.at[turn, stage], a_recv.at[turn, stage], peer).start()
-            sent.append((landed.at[turn], a_send.at[turn, stage]))
-            after = (after_first, after_second)[stage]
+                remote(arow.at[turn, stage], landed.at[k], a_send.at[turn, stage], a_recv.at[turn, stage], peer).start()
+            sent.append((landed, a_send.at[turn, stage]))
             if after is not None:
                 after()
-            settle(landed.at[turn], a_recv.at[turn, stage])
-            row = tree([row] + [landed[turn, k] for k in range(len(peers))])
+            settle(landed, a_recv.at[turn, stage])
+            row = tree([row] + [landed[k] for k in range(len(peers))])
         return row
 
     xs = [lax.rem(x + dx, X) for dx in range(X)]
@@ -155,17 +155,13 @@
     ch_at = [[(py // Y_LO) * Z + pz for pz in zs] for py in ys]
 
     def all_sum_direct(row):
-        arow[1, 0] = row
-        pair, landed = arecv_all.at[pl.ds(len(EVERYONE), 1)], arecv_all.at[pl.ds(0, len(EVERYONE))]
-        remote(arow.at[1, pl.ds(0, 1)], pair, all_send.at[0], all_recv.at[0], sibling).start()
-        settle(pair, all_recv.at[0])
-        row = row + arecv_all[len(EVERYONE)]
+        row = all_sum(1, [([sibling], arecv_p, drain)], row)
+        landed = arecv_all
         arow[1, 1] = row
         for k, (dx, dy, dz) in enumerate(EVERYONE):
-            remote(arow.at[1, 1], arecv_all.at[k], all_send.at[1], all_recv.at[1], (ev_at[dx][dy], ch_at[dy][dz])).start()
-        sent.append((pair, all_send.at[0]))
-        sent.append((landed, all_send.at[1]))
-        settle(landed, all_recv.at[1])
+            remote(arow.at[1, 1], arecv_all.at[k], all_send.at[0], all_recv.at[0], (ev_at[dx][dy], ch_at[dy][dz])).start()
+        sent.append((landed, all_send.at[0]))
+        settle(landed, all_recv.at[0])
         return tree([row] + [arecv_all[k] for k in range(len(EVERYONE))])
 
     for copy in small[:-1]:
@@ -229,10 +225,12 @@
                     sums[...] = acc[0] + acc[1]
         row = to_row(jnp.sum(sums[...], axis=1, keepdims=True))
         row = jnp.where(lanes[0:1] == freqs, count, row)
-        drain()
         if it == 0:
-            pl.semaphore_wait(barrier, len(stage_a) + len(stage_b))
-        total = all_sum(0, row) if it == 0 else all_sum_direct(row)
+            pl.semaphore_wait(barrier, len(greeted))
+        if it == 0:
+            total = all_sum(0, ((stage_a, arecv_a.at[0], None), (stage_b, arecv_b.at[0], None)), row)
+        else:
+            total = all_sum_direct(row)
         number = jnp.sum(jnp.where(lanes[0:1] == freqs, total, 0.0), axis=1, keepdims=True)
         mean = to_column(total) / jnp.maximum(jnp.broadcast_to(number, (freqs, 1)), 1.0)
         limit = jnp.broadcast_to(1.345 * (1.2533 * mean + 1e-05), shape)
@@ -303,6 +301,10 @@
                 peer = (x * Y_LO + row_of(i)) * CORE + core
                 remote(ysend.at[it, i], recv_y.at[it, slot], y_send.at[0], y_recv.at[0], (peer, ch)).start()
         sent.append((recv_y.at[it], y_send.at[0]))
+        settle(brecv.at[it], b_recv.at[0])
+        bsend[it, 1] = tree([bsend[it, 0]] + [brecv[it, k] for k in range(len(along_z))])
+        remote(bsend.at[it, 1], brecv2.at[it], b_send.at[1], b_recv.at[1], across_y).start()
+        sent.append((brecv2.at[it], b_send.at[1]))
         settle(recv_y.at[it], y_recv.at[0])
         both = tree([both] + [recv_y[it, i] for i in range(Y_LO - 1)])
         tile = core * half + chip
@@ -324,12 +326,6 @@
             sent.append((gath.at[it, pl.ds(0, others)], g_send.at[0]))
             sent.append((gath.at[it, pl.ds(0, half)], f_send.at[0]))
 
-        def across():
-            settle(brecv.at[it], b_recv.at[0])
-            bsend[it, 1] = tree([bsend[it, 0]] + [brecv[it, k] for k in range(len(along_z))])
-            remote(bsend.at[it, 1], brecv2.at[it], b_send.at[1], b_recv.at[1], across_y).start()
-            sent.append((brecv2.at[it], b_send.at[1]))
-
         def source_rest():
             settle(brecv2.at[it], b_recv.at[1])
             both = bsend[it, 1] + brecv2[it]
@@ -342,7 +338,7 @@
                 srcb[e] += dsb[e]
 
         def forward():
-            for batch, (first, last) in enumerate(((0, NEAR), (NEAR, others))):
+            for batch, first, last in ((1, NEAR, others), (0, 0, NEAR)):
                 settle(gath.at[it, pl.ds(0, last - first)], g_recv.at[batch])
                 for p in range(first, last):
                     come = core * half + chip_from(p)
@@ -350,27 +346,27 @@
 
         if it < ITERS - 1:
             gather()
-            across()
+            source_rest()
             forward()
-            source_rest()
         else:
-            def meanwhile():
-                across()
+            def finish():
                 forward()
-            total = all_sum(2, last_row, gather, meanwhile) * (1.0 / (n_ch * Y_HI * Z))
-            source_rest()
-            settle(gath.at[it, pl.ds(0, half)], f_recv.at[0])
+                source_rest()
+                for e in range(n_ev):
+                    out = to_row(srcb[e][:, 0:1])
+                    source_o[e:e + 1, :] = out[:, 0:freqs]
+                settle(gath.at[it, pl.ds(0, half)], f_recv.at[0])
+                for t in range(tiles):
+                    at = slice(t * LANES, (t + 1) * LANES)
+                    site_o[:, at] = tree([site[:, at]] + [gath[i, t] for i in range(ITERS)])
+            stages = (stage_a, arecv_a.at[1], gather), (stage_b, arecv_b.at[1], finish)
+            total = all_sum(2, stages, last_row) * (1.0 / (n_ch * Y_HI * Z))
 
     shift = jnp.broadcast_to(to_column(total), shape)
     for t in range(tiles):
         at = slice(t * LANES, (t + 1) * LANES)
-        out = site[:, at]
-        for i in range(ITERS):
-            out = out + gath[i, t]
-        site_o[:, at] = out - shift
-    for e in range(n_ev):
-        out = to_row(srcb[e][:, 0:1]) + total
-        source_o[e:e + 1, :] = out[:, 0:freqs]
+        site_o[:, at] = site_o[:, at] - shift
+    source_o[...] = source_o[...] + jnp.broadcast_to(total[:, 0:freqs], (n_ev, freqs))
     drain()
 
 
@@ -402,10 +398,10 @@
         v((ITERS, Y_LO, X - 1, 2) + block, f32), v((ITERS, Y_LO - 1, 2) + block, f32), v((ITERS, Y_LO - 1, 2) + block, f32),
         v((ITERS, tiles) + block, f32),
         v((ITERS, 2, 8, LANES), f32), v((ITERS, Z - 1, 8, LANES), f32), v((ITERS, 8, LANES), f32),
-        v((ITERS + 1, 2, 1, LANES), f32), v((ITERS + 1, na, 1, LANES), f32), v((ITERS + 1, nb, 1, LANES), f32),
-        v((len(EVERYONE) + 1, 1, LANES), f32),
+        v((ITERS + 1, 2, 1, LANES), f32), v((1, 1, LANES), f32),
+        v((2, na, 1, LANES), f32), v((2, nb, 1, LANES), f32), v((len(EVERYONE), 1, LANES), f32),
         dma((4,)), dma((7,)), dma((1,)), dma((Y_LO,)), dma((1,)), dma((Y_LO,)), dma((1,)), dma((1,)),
-        dma((1,)), dma((2,)), dma((1,)), dma((1,)), dma((2,)), dma((2,)), dma((ITERS + 1, 2)), dma((ITERS + 1, 2)), dma((2,)), dma((2,)),
+        dma((1,)), dma((2,)), dma((1,)), dma((1,)), dma((2,)), dma((2,)), dma((ITERS + 1, 2)), dma((ITERS + 1, 2)), dma((1,)), dma((1,)),
     ]
     hbm = pl.BlockSpec(memory_space=pltpu.HBM)
     vmem = pl.BlockSpec(memory_space=pltpu.VMEM)

time: 72.9 us -> 72.7 us (level)
  no operation moved by 1% of the time
where the time goes in v4:
time: 72.7 us; the launch traced here: 72.5 us
  Pallas kernels  71.9 us (99%)
    pallas_call x1, Pallas kernels, on_device(): pl.pallas_call(kernel, out_shape=tuple((pltpu.VMEM(v.shape, f32) for v in...  71.1 us

profile of v4, /device:TPU:1, one launch (start us, length us, event | category | flops | bytes accessed | tf_op | source)
XLA Modules:
  0.0 72.5 jit_solution(7477848369578363304)
XLA Ops:
  0.6 71.1 %estimate.1 = (f32[16,16]{1,0:T(8,128)S(1)}, f32[16,4096]{1,0:T(8,128)S(1)}) custom-call(f32[16,16,4096]{2,1,0:T(8,128)} %spectra.1, s32[16,32]{1,0:T(8,128)} %mask_h.1, f32[16,16]{1,0:T(8,128)} %source_h.1, f32[16,4096]{1,0:T(8,128)} %site_h.1, f32[3,16]{1,0:T(4,128)} %event_h.1, f32[2,4096]{1,0:T(2,128)} %channel_h.1, f32[1,16]{1,0:T(1,128)} %bitcast.1), custom_call_target="tpu_custom_call" | custom-call | tf_op jit(solution)/shard_map/estimate/pallas_call | solution.py:410
  71.8 0.7 %store.1 = (f32[16,16]{1,0:T(8,128)}, f32[16,4096]{1,0:T(8,128)}) custom-call(f32[16,16]{1,0:T(8,128)S(1)} %get-tuple-element.4.source, f32[16,4096]{1,0:T(8,128)S(1)} %get-tuple-element.5.site), custom_call_target="tpu_custom_call" | custom-call | tf_op jit(solution)/shard_map/store/pallas_call | solution.py:421

commit v5 on v4

--- a/solution.py
+++ b/solution.py
@@ -31,11 +31,6 @@
     key=lambda s: -ring(s[0], X) - ring(s[1], Y) - ring(s[2], Z),
 )
 NEAR = 8
-
-
-def group_step(p):
-    i = p // X
-    return (p % X + 1) % X, (2 + i + i * (i - 1) // 2) % Y_LO
 
 
 def kernel(
@@ -75,12 +70,14 @@
     across_x = [lax.rem(x + j + 1, X) * Y_LO for j in range(X)]
 
     def chip_at(p):
-        dx, dy = group_step(p)
-        return lax.rem(x + dx, X) * Y_LO + lax.rem(y_lo + dy, Y_LO)
+        return across_x[p % X] + row_of(p // X)
 
     def chip_from(p):
-        dx, dy = group_step(p)
-        return lax.rem(x + X - dx, X) * Y_LO + lax.rem(y_lo + Y_LO - dy, Y_LO)
+        if p < NEAR:
+            return p // 2 * Y_LO + 2 * (1 - upper) + p % 2
+        if p < NEAR + X:
+            return (p - NEAR) * Y_LO + y_lo + 1 - 2 * lax.rem(y_lo, 2)
+        return across_x[p - NEAR - X] + y_lo
 
     barrier = pltpu.get_barrier_semaphore()
     greeted = stage_b + stage_a

time: 72.7 us -> 72.6 us (level)
  no operation moved by 1% of the time
where the time goes in v5:
time: 72.6 us; the launch traced here: 72.5 us
  Pallas kernels  71.8 us (99%)
    pallas_call x1, Pallas kernels, on_device(): pl.pallas_call(kernel, out_shape=tuple((pltpu.VMEM(v.shape, f32) for v in...  71.1 us

profile of v5, /device:TPU:1, one launch (start us, length us, event | category | flops | bytes accessed | tf_op | source)
XLA Modules:
  0.0 72.5 jit_solution(4155673398050549853)
XLA Ops:
  0.6 71.1 %estimate.1 = (f32[16,16]{1,0:T(8,128)S(1)}, f32[16,4096]{1,0:T(8,128)S(1)}) custom-call(f32[16,16,4096]{2,1,0:T(8,128)} %spectra.1, s32[16,32]{1,0:T(8,128)} %mask_h.1, f32[16,16]{1,0:T(8,128)} %source_h.1, f32[16,4096]{1,0:T(8,128)} %site_h.1, f32[3,16]{1,0:T(4,128)} %event_h.1, f32[2,4096]{1,0:T(2,128)} %channel_h.1, f32[1,16]{1,0:T(1,128)} %bitcast.1), custom_call_target="tpu_custom_call" | custom-call | tf_op jit(solution)/shard_map/estimate/pallas_call | solution.py:407
  71.8 0.7 %store.1 = (f32[16,16]{1,0:T(8,128)}, f32[16,4096]{1,0:T(8,128)}) custom-call(f32[16,16]{1,0:T(8,128)S(1)} %get-tuple-element.4.source, f32[16,4096]{1,0:T(8,128)S(1)} %get-tuple-element.5.site), custom_call_target="tpu_custom_call" | custom-call | tf_op jit(solution)/shard_map/store/pallas_call | solution.py:418

commit v6 on v5

--- a/solution.py
+++ b/solution.py
@@ -36,7 +36,7 @@
 def kernel(
     spectra, mask_h, source_h, site_h, event_h, channel_h, atten_h,
     source_o, site_o,
-    rbuf, site, chan, srcv, attv, maskv, mask, evp, chx, srcb, dsb, sn, sd, sums,
+    rbuf, site, chan, srcv, attv, maskv, mask, evp, chx, srcb, dsb, sn, sd, sums, kept,
     away, recv_s, own, recv_x, ysend, recv_y, gath, bsend, brecv, brecv2, arow, arecv_p, arecv_a, arecv_b, arecv_all,
     spec_sem, in_sem, s_send, s_recv, x_send, x_recv, y_send, y_recv, g_send, g_recv, f_send, f_recv,
     b_send, b_recv, a_send, a_recv, all_send, all_recv,
@@ -181,6 +181,12 @@
 
     small[-1].wait()
     zero = jnp.zeros(shape, f32)
+
+    def spread_mask():
+        flags = maskv[...].astype(f32)
+        for t in range(tiles):
+            kept[t] = jnp.broadcast_to(flags[:, t:t + 1], (n_ev, LANES))
+
     for it in range(ITERS):
         def first(e, carry):
             accs = list(carry)
@@ -225,7 +231,7 @@
         if it == 0:
             pl.semaphore_wait(barrier, len(greeted))
         if it == 0:
-            total = all_sum(0, ((stage_a, arecv_a.at[0], None), (stage_b, arecv_b.at[0], None)), row)
+            total = all_sum(0, ((stage_a, arecv_a.at[0], spread_mask), (stage_b, arecv_b.at[0], None)), row)
         else:
             total = all_sum_direct(row)
         number = jnp.sum(jnp.where(lanes[0:1] == freqs, total, 0.0), axis=1, keepdims=True)
@@ -245,7 +251,7 @@
                     num = den = None
                     for u, t in enumerate(where):
                         r = rbuf[e, :, pl.ds(pl.multiple_of(t * LANES, LANES), LANES)]
-                        w = limit * mask[e, t].astype(f32) / jnp.maximum(jnp.abs(r), limit)
+                        w = limit * jnp.broadcast_to(kept[t, e:e + 1, :], shape) / jnp.maximum(jnp.abs(r), limit)
                         p = w * r
                         totals[2 * u] += p
                         totals[2 * u + 1] += w
@@ -390,7 +396,7 @@
         v((1, freqs), f32), v((n_ev, tiles), jnp.int32),
         pltpu.SMEM((n_ev, tiles), jnp.int32), pltpu.SMEM((3, n_ev), f32),
         v((2, tiles, LANES), f32), v((n_ev,) + block, f32), v((n_ev,) + block, f32),
-        v((n_ev,) + block, f32), v((n_ev,) + block, f32), v(block, f32),
+        v((n_ev,) + block, f32), v((n_ev,) + block, f32), v(block, f32), v((tiles, n_ev, LANES), f32),
         v((ITERS, half, 2) + block, f32), v((ITERS, half, 2) + block, f32), v((ITERS, half, 2) + block, f32),
         v((ITERS, Y_LO, X - 1, 2) + block, f32), v((ITERS, Y_LO - 1, 2) + block, f32), v((ITERS, Y_LO - 1, 2) + block, f32),
         v((ITERS, tiles) + block, f32),

time: 72.6 us -> 72.6 us (level)
  no operation moved by 1% of the time
where the time goes in v6:
time: 72.6 us; the launch traced here: 72.5 us
  Pallas kernels  71.8 us (99%)
    pallas_call x1, Pallas kernels, on_device(): pl.pallas_call(kernel, out_shape=tuple((pltpu.VMEM(v.shape, f32) for v in...  71.1 us

profile of v6, /device:TPU:1, one launch (start us, length us, event | category | flops | bytes accessed | tf_op | source)
XLA Modules:
  0.0 72.5 jit_solution(8062220169723617557)
XLA Ops:
  0.6 71.1 %estimate.1 = (f32[16,16]{1,0:T(8,128)S(1)}, f32[16,4096]{1,0:T(8,128)S(1)}) custom-call(f32[16,16,4096]{2,1,0:T(8,128)} %spectra.1, s32[16,32]{1,0:T(8,128)} %mask_h.1, f32[16,16]{1,0:T(8,128)} %source_h.1, f32[16,4096]{1,0:T(8,128)} %site_h.1, f32[3,16]{1,0:T(4,128)} %event_h.1, f32[2,4096]{1,0:T(2,128)} %channel_h.1, f32[1,16]{1,0:T(1,128)} %bitcast.1), custom_call_target="tpu_custom_call" | custom-call | tf_op jit(solution)/shard_map/estimate/pallas_call | solution.py:413
  71.7 0.7 %store.1 = (f32[16,16]{1,0:T(8,128)}, f32[16,4096]{1,0:T(8,128)}) custom-call(f32[16,16]{1,0:T(8,128)S(1)} %get-tuple-element.4.source, f32[16,4096]{1,0:T(8,128)S(1)} %get-tuple-element.5.site), custom_call_target="tpu_custom_call" | custom-call | tf_op jit(solution)/shard_map/store/pallas_call | solution.py:424
